TPU v7x, 256 devices: a whole 4x4x8 slice. The times are simulated.
256 devices in a mesh: rows: 32 (over y, x, core), cols: 8 (over z).
Axes of the slice: x: 4, y: 4, z: 8, core: 2. Of those that a mesh axis runs over, the one named last changes fastest.
Arguments:
- owner_map: int32 [2, 512], replicated, may hold values from 0 to 511, as said below
- colidx: int32 [2, 512, 24], P(None, 'rows', 'cols'), may hold values from 0 to 767, as said below
- live: int32 [2, 512], P(None, 'rows'), may hold values from 1 to 24
- blocks: bfloat16 [2, 512, 24, 128, 128], P(None, 'rows', 'cols'), may hold values from -0.15625 to 0.15625
- diag_inverse: float32 [2, 512, 128, 128], P(None, 'rows')
- right_side: float32 [2, 512, 64, 128], P(None, 'rows'), may hold values from -6 to 6
- prior: bfloat16 [256, 64, 128], P('rows'), may hold values from -6 to 6
Outputs:
- solved: float32 [2, 512, 64, 128], P(None, 'rows')
Inputs may be any that keep to these rules, and one draw needn't show every extreme that they name: Each row of owner_map is a permutation of the block rows of a front. `colidx`: front 0 refers only to earlier block rows; in front 1, even slots refer to rows of front 0 and odd slots to earlier block rows. Take the even slots of front 1 that lie in block rows s with s // 16 equal to one value and in slots j with j // 3 equal to one value. Among them, at most 1 refer to front-0 rows r whose slot t (owner_map[0, t] = r) has t // 16 equal to any single value; some such group reaches 1.
All inputs are finite; a program needn't handle non-finite values.
Results may differ from a plain program's by a relative error of at most 0.0017.
Values may be sent and summed in bfloat16 or wider, within the bound.
A program may use at most 64 MiB of HBM per device.

v0:
```python
import jax
import jax.numpy as jnp
from jax import lax
from jax.sharding import PartitionSpec as P


def solve_diag(resid, inverse):
    return jnp.einsum(
        "rpb,rcb->rpc",
        resid,
        inverse,
        precision=lax.Precision.HIGHEST,
        preferred_element_type=jnp.float32,
    )


def block_products(blk, values):
    return jnp.einsum("rjcb,rjpb->rpc", blk, values, preferred_element_type=jnp.float32)


def finish(partial_value, rhs_front, inverse):
    total = lax.psum(partial_value, "cols")
    return solve_diag(rhs_front - total, inverse)


def shards(owner_map, colidx, live, blocks, diag_inverse, right_side, prior):
    slot_count = blocks.shape[2]
    col_here = lax.axis_index("cols")
    rows_front = owner_map.shape[1]
    slot_ids = col_here * slot_count + jnp.arange(slot_count, dtype=jnp.int32)
    live_mask = slot_ids[None, None, :] < live[:, :, None]
    prior_all = lax.all_gather(prior, "rows", axis=0, tiled=True)
    prior_count = prior_all.shape[0]
    zero_value = jnp.zeros((), jnp.bfloat16)
    first_idx = jnp.clip(colidx[0], 0, prior_count - 1)
    first_values = jnp.where(live_mask[0][:, :, None, None], prior_all[first_idx], zero_value)
    first = finish(block_products(blocks[0], first_values), right_side[0], diag_inverse[0])
    first_low = first.astype(jnp.bfloat16)
    second_idx = colidx[1]
    from_prior = second_idx < prior_count
    inverse_map = (
        jnp.zeros((rows_front,), jnp.int32)
        .at[owner_map[0]]
        .set(jnp.arange(rows_front, dtype=jnp.int32))
    )
    slot_pos = inverse_map[jnp.clip(second_idx - prior_count, 0, rows_front - 1)]
    whole_front = lax.all_gather(first_low, "rows", axis=0, tiled=True)
    recent_values = whole_front[slot_pos]
    early_values = prior_all[jnp.clip(second_idx, 0, prior_count - 1)]
    chosen = jnp.where(from_prior[:, :, None, None], early_values, recent_values)
    second_values = jnp.where(live_mask[1][:, :, None, None], chosen, zero_value)
    second = finish(block_products(blocks[1], second_values), right_side[1], diag_inverse[1])
    return jnp.stack([first, second])


def solution(mesh):
    placed = (
        P(),
        P(None, "rows", "cols"),
        P(None, "rows"),
        P(None, "rows", "cols", None, None),
        P(None, "rows", None, None),
        P(None, "rows", None, None),
        P("rows", None, None),
    )
    return jax.shard_map(
        shards, mesh=mesh, in_specs=placed, out_specs=P(None, "rows", None, None), check_vma=False
    )
```

profile of v0, /device:TPU:2, one launch (start us, length us, event | category | flops | bytes accessed | tf_op | source)
XLA Modules:
  0.0 295.8 jit_solution(2289434202157852496)
XLA Ops:
  6.5 0.0 copy-start
  6.5 0.0 all-gather.3.cloned.1.call-start
  6.5 0.7 all-gather.3.cloned.1.call-update
  7.3 0.0 all-reduce.3.cloned.1.call-start
  7.3 0.8 compare_select_fusion.2
  8.1 0.1 copy.29
  8.2 0.1 reshape.128
  8.3 0.8 broadcast_compare_fusion
  9.0 0.1 copy.28
  9.1 54.5 %all-gather.3.cloned.1.call-done = bf16[256,64,128]{2,1,0:T(8,128)(2,1)} async-done(((bf16[8,64,128]{2,1,0:T(8,128)(2,1)}), bf16[256,64,128]{2,1,0:T(8,128)(2,1)}) %all-gather.3.cloned.1.call-update) | async-done | bytes 4194320 | tf_op jit(solution)/shard_map/all_gather | solution.py:32
  63.7 2.9 gather_fusion
  66.6 0.0 copy-start.2
  66.6 3.0 %fusion.6 = f32[16,64,128]{2,1,0:T(8,128)} fusion(bf16[2,16,3,128,128]{4,3,2,1,0:T(8,128)(2,1)} %param.10, bf16[16,3,64,128]{3,2,1,0:T(8,128)(2,1)S(1)} %bitcast.63, pred[16,3]{1,0:T(8,128)(4,1)S(1)} %copy.28), kind=kOutput, calls=%fused_computation.11 | convolution fusion | flops 101056512 | bytes 2883632 | tf_op jit(solution)/shard_map/rjcb,rjpb->rpc/dot_general | solution.py:18
  69.6 0.0 all-reduce.3.cloned.1.call-update
  69.6 0.0 all-gather.5.cloned.1.call-start
  69.7 73.2 %all-reduce.3.cloned.1.call-done = f32[16,64,128]{2,1,0:T(8,128)} async-done(((f32[16,64,128]{2,1,0:T(8,128)}), f32[16,64,128]{2,1,0:T(8,128)}) %all-reduce.3.cloned.1.call-update) | async-done | bytes 524304 | tf_op jit(solution)/shard_map/psum | solution.py:22
  142.9 0.0 copy-done
  142.9 4.0 %fusion.31 = (bf16[16,64,128]{2,1,0:T(8,128)(2,1)}, f32[16,64,128]{2,1,0:T(8,128)S(1)}) fusion(f32[2,16,128,128]{3,2,1,0:T(8,128)S(1)} %copy-done, f32[16,64,128]{2,1,0:T(8,128)} %all-reduce.3.cloned.1.call-done, f32[2,16,64,128]{3,2,1,0:T(8,128)} %param.12), kind=kOutput, calls=%fused_computation.50 | convolution fusion | flops 201588736 | bytes 2883584 | tf_op jit(solution)/shard_map/rpb,rcb->rpc/dot_general | solution.py:8
  147.0 0.0 all-gather.5.cloned.1.call-update
  147.0 0.0 all-reduce.5.cloned.1.call-start
  147.0 0.1 copy.32
  147.1 0.1 reshape.136
  147.2 0.1 copy.33
  147.3 0.1 reshape.144
  147.4 0.0 copy-done.2
  147.4 2.4 scatter_custom_fusion
  149.9 0.0 copy-start.1
  149.9 0.8 gather_fusion.2
  150.7 0.1 gather.17
  150.8 0.1 copy.34
  150.9 0.1 copy.37
  150.9 0.1 reshape.152
  151.1 0.0 copy-done.1
  151.1 0.1 copy.40
  151.2 0.1 copy.30
  151.3 2.9 gather_fusion.1
  154.2 49.3 %all-gather.5.cloned.1.call-done = bf16[512,64,128]{2,1,0:T(8,128)(2,1)} async-done(((bf16[16,64,128]{2,1,0:T(8,128)(2,1)}), bf16[512,64,128]{2,1,0:T(8,128)(2,1)}) %all-gather.5.cloned.1.call-update) | async-done | bytes 8388624 | tf_op jit(solution)/shard_map/all_gather | solution.py:47
  203.5 4.9 %gather_fusion.3 = bf16[48,64,128]{2,1,0:T(8,128)(2,1)} fusion(bf16[512,64,128]{2,1,0:T(8,128)(2,1)} %all-gather.5.cloned.1.call-done, s32[1024]{0:T(1024)S(1)} %pad_clamp_fusion), kind=kCustom, calls=%fused_computation.3 | custom fusion | bytes 1573056 | tf_op jit(solution)/shard_map/gather | solution.py:48
  208.4 3.3 %fusion.9 = f32[16,64,128]{2,1,0:T(8,128)} fusion(bf16[2,16,3,128,128]{4,3,2,1,0:T(8,128)(2,1)} %param.10, bf16[16,3,64,128]{3,2,1,0:T(8,128)(2,1)S(1)} %bitcast.61, bf16[16,3,64,128]{3,2,1,0:T(8,128)(2,1)} %bitcast.62, pred[16,3]{1,0:T(8,128)(4,1)S(1)} %bitcast.64, pred[16,3]{1,0:T(8,128)(4,1)S(1)} %copy.30), kind=kOutput, calls=%fused_computation.12 | convolution fusion | flops 101449728 | bytes 3670112 | tf_op jit(solution)/shard_map/rjcb,rjpb->rpc/dot_general | solution.py:18
  211.7 0.0 all-reduce.5.cloned.1.call-update
  211.7 73.2 %all-reduce.5.cloned.1.call-done = f32[16,64,128]{2,1,0:T(8,128)} async-done(((f32[16,64,128]{2,1,0:T(8,128)}), f32[16,64,128]{2,1,0:T(8,128)}) %all-reduce.5.cloned.1.call-update) | async-done | bytes 524304 | tf_op jit(solution)/shard_map/psum | solution.py:22
  284.9 3.3 %convolution_bitcast_fusion = f32[1,16,64,128]{3,2,1,0:T(8,128)S(1)} fusion(f32[2,16,128,128]{3,2,1,0:T(8,128)S(1)} %copy-done, f32[16,64,128]{2,1,0:T(8,128)} %all-reduce.5.cloned.1.call-done, f32[2,16,64,128]{3,2,1,0:T(8,128)} %param.12), kind=kOutput, calls=%fused_computation.13 | convolution fusion | flops 201457664 | bytes 2621440 | tf_op jit(solution)/shard_map/rpb,rcb->rpc/dot_general | solution.py:8
  288.2 1.1 pad_maximum_fusion
  (10 shorter events, 0.1 us)
Async XLA Ops:
  6.5 136.4 %copy-start = (f32[2,16,128,128]{3,2,1,0:T(8,128)S(1)}, f32[2,16,128,128]{3,2,1,0:T(8,128)}, u32[]{:S(2)}) copy-start(f32[2,16,128,128]{3,2,1,0:T(8,128)} %param.11) | copy-start | bytes 6291460
  6.5 57.1 %all-gather.3.cloned.1.call-start = ((), (), s32[]{:S(2)}) async-start(), calls=%async_computation | async-start | bytes 4325376 | tf_op jit(solution)/shard_map/all_gather | solution.py:32
  7.3 135.7 %all-reduce.3.cloned.1.call-start = ((), (), s32[]{:S(2)}) async-start(), calls=%async_computation.1 | async-start | bytes 1048576 | tf_op jit(solution)/shard_map/psum | solution.py:22
  66.6 80.8 %copy-start.2 = (s32[2,512]{1,0:T(2,128)S(1)}, s32[2,512]{1,0:T(2,128)}, u32[]{:S(2)}) copy-start(s32[2,512]{1,0:T(2,128)} %param.7) | copy-start | bytes 12292
  69.6 133.8 %all-gather.5.cloned.1.call-start = ((), (), s32[]{:S(2)}) async-start(), calls=%async_computation.2 | async-start | bytes 8650752 | tf_op jit(solution)/shard_map/all_gather | solution.py:47
  147.0 137.9 %all-reduce.5.cloned.1.call-start = ((), (), s32[]{:S(2)}) async-start(), calls=%async_computation.3 | async-start | bytes 1048576 | tf_op jit(solution)/shard_map/psum | solution.py:22
  149.9 1.2 copy-start.1
Sparse Core Ops, SparseCore 0:
  9.9 53.7 all-gather.2
  69.8 73.1 all-reduce.2
  147.1 56.3 all-gather.4
  211.9 73.0 all-reduce.4
where the time goes:
time: 296 us
  waiting for transfers between devices  251 us (85%)
  local copies, waits for them, and re-layouts  15.1 us (5%)
  matrix products  13.7 us (5%)
  between operations  13.3 us (4%)
    psum x2, waiting for transfers between devices, finish(): total = lax.psum(partial_value, 'cols')  146 us
    all_gather x1, waiting for transfers between devices, shards(): prior_all = lax.all_gather(prior, 'rows', axis=0, tiled=True)  54.5 us
    all_gather x1, waiting for transfers between devices, shards(): whole_front = lax.all_gather(first_low, 'rows', axis=0, tiled=True)  49.3 us
    dot_general x2, matrix products, solve_diag(): jnp.einsum('rpb,rcb->rpc', resid, inverse, precision=lax.Precision.HIGHES...  7.34 us
    dot_general x2, matrix products, block_products(): jnp.einsum('rjcb,rjpb->rpc', blk, values, preferred_element_type=jnp.floa...  6.37 us
  transfers between devices with their start and end apart: 4, of which 4 were waited for; matrix products, arithmetic and copies ran while one was open for 3% of the time, Pallas kernels for 0%

commit v1 on v0

--- a/solution.py
+++ b/solution.py
@@ -19,7 +19,7 @@
 
 
 def finish(partial_value, rhs_front, inverse):
-    total = lax.psum(partial_value, "cols")
+    total = jnp.sum(lax.all_gather(partial_value, "cols"), axis=0)
     return solve_diag(rhs_front - total, inverse)
 
 

time: 296 us -> 265 us (0.90)
  waiting for transfers between devices: 251 us -> 214 us
  other arithmetic: 2.64 us -> 7.85 us
    psum x2 -> x0, waiting for transfers between devices: 146 us -> none  [finish(): total = lax.psum(partial_value, 'cols')]
    all_gather x0 -> x2, waiting for transfers between devices: none -> 109 us  [finish(): total = jnp.sum(lax.all_gather(partial_value, 'cols'), axis=0)]
    reduce_sum x0 -> x2, other arithmetic: none -> 5.22 us  [finish(): total = jnp.sum(lax.all_gather(partial_value, 'cols'), axis=0)]
where the time goes in v1:
time: 265 us; the launch traced here: 264 us
  waiting for transfers between devices  214 us (81%)
  local copies, waits for them, and re-layouts  15.1 us (6%)
  matrix products  13.4 us (5%)
  between operations  13.3 us (5%)
  other arithmetic  7.85 us (3%)
    all_gather x2, waiting for transfers between devices, finish(): total = jnp.sum(lax.all_gather(partial_value, 'cols'), axis=0)  109 us
    all_gather x1, waiting for transfers between devices, shards(): prior_all = lax.all_gather(prior, 'rows', axis=0, tiled=True)  54.5 us
    all_gather x1, waiting for transfers between devices, shards(): whole_front = lax.all_gather(first_low, 'rows', axis=0, tiled=True)  49.5 us
    dot_general x2, matrix products, solve_diag(): jnp.einsum('rpb,rcb->rpc', resid, inverse, precision=lax.Precision.HIGHES...  7.03 us
    dot_general x2, matrix products, block_products(): jnp.einsum('rjcb,rjpb->rpc', blk, values, preferred_element_type=jnp.floa...  6.39 us
  transfers between devices with their start and end apart: 4, of which 4 were waited for; matrix products, arithmetic and copies ran while one was open for 3% of the time, Pallas kernels for 0%

profile of v1, /device:TPU:2, one launch (start us, length us, event | category | flops | bytes accessed | tf_op | source)
XLA Modules:
  0.0 263.8 jit_solution(17476752351465339239)
XLA Ops:
  6.5 0.0 all-gather.7.cloned.1.call-start
  6.5 0.7 all-gather.7.cloned.1.call-update
  7.3 0.0 all-gather.11.cloned.1.call-start
  7.3 0.8 compare_select_fusion.2
  8.1 0.1 copy.29
  8.2 0.1 reshape.128
  8.3 0.8 broadcast_compare_fusion
  9.0 0.1 copy.28
  9.1 54.5 %all-gather.7.cloned.1.call-done = bf16[256,64,128]{2,1,0:T(8,128)(2,1)} async-done(((bf16[8,64,128]{2,1,0:T(8,128)(2,1)}), bf16[256,64,128]{2,1,0:T(8,128)(2,1)}) %all-gather.7.cloned.1.call-update) | async-done | bytes 4194320 | tf_op jit(solution)/shard_map/all_gather | solution.py:32
  63.7 2.9 %gather_fusion = bf16[48,64,128]{2,1,0:T(8,128)(2,1)S(1)} fusion(bf16[256,64,128]{2,1,0:T(8,128)(2,1)} %all-gather.7.cloned.1.call-done, s32[1024]{0:T(1024)S(1)} %pad_clamp_fusion.3), kind=kCustom, calls=%fused_computation | custom fusion | bytes 1573056 | tf_op jit(solution)/shard_map/gather | solution.py:36
  66.6 3.0 %fusion.6 = f32[16,64,128]{2,1,0:T(8,128)} fusion(bf16[2,16,3,128,128]{4,3,2,1,0:T(8,128)(2,1)} %param.10, bf16[16,3,64,128]{3,2,1,0:T(8,128)(2,1)S(1)} %bitcast.67, pred[16,3]{1,0:T(8,128)(4,1)S(1)} %copy.28), kind=kOutput, calls=%fused_computation.11 | convolution fusion | flops 101056512 | bytes 2883632 | tf_op jit(solution)/shard_map/rjcb,rjpb->rpc/dot_general | solution.py:18
  69.6 0.0 copy-start
  69.6 0.0 all-gather.11.cloned.1.call-update
  69.6 0.0 all-gather.9.cloned.1.call-start
  69.7 54.7 %all-gather.11.cloned.1.call-done = f32[128,64,128]{2,1,0:T(8,128)} async-done(((f32[16,64,128]{2,1,0:T(8,128)}), f32[128,64,128]{2,1,0:T(8,128)}) %all-gather.11.cloned.1.call-update) | async-done | bytes 4194320 | tf_op jit(solution)/shard_map/all_gather | solution.py:22
  124.4 0.0 copy-start.2
  124.4 2.6 reduce_sum.18
  127.0 0.0 copy-done
  127.0 3.9 %fusion.31 = (bf16[16,64,128]{2,1,0:T(8,128)(2,1)}, f32[16,64,128]{2,1,0:T(8,128)S(1)}) fusion(f32[2,16,128,128]{3,2,1,0:T(8,128)S(1)} %copy-done, f32[16,64,128]{2,1,0:T(8,128)S(1)} %reduce_sum.18, f32[2,16,64,128]{3,2,1,0:T(8,128)} %param.12), kind=kOutput, calls=%fused_computation.50 | convolution fusion | flops 201588736 | bytes 2883584 | tf_op jit(solution)/shard_map/rpb,rcb->rpc/dot_general | solution.py:8
  130.9 0.0 all-gather.9.cloned.1.call-update
  130.9 0.0 all-gather.13.cloned.1.call-start
  130.9 0.1 copy.32
  131.0 0.1 reshape.136
  131.1 0.1 copy.33
  131.2 0.1 reshape.144
  131.3 0.0 copy-done.2
  131.3 2.4 scatter_custom_fusion
  133.8 0.0 copy-start.1
  133.8 0.8 gather_fusion.2
  134.6 0.1 gather.17
  134.7 0.1 copy.34
  134.8 0.1 copy.37
  134.8 0.1 reshape.152
  134.9 0.0 copy-done.1
  135.0 0.1 copy.40
  135.1 0.1 copy.30
  135.2 2.9 %gather_fusion.1 = bf16[48,64,128]{2,1,0:T(8,128)(2,1)S(1)} fusion(bf16[256,64,128]{2,1,0:T(8,128)(2,1)} %all-gather.7.cloned.1.call-done, s32[1024]{0:T(1024)S(1)} %pad_clamp_fusion.2), kind=kCustom, calls=%fused_computation.1 | custom fusion | bytes 1573056 | tf_op jit(solution)/shard_map/gather | solution.py:49
  138.1 49.5 %all-gather.9.cloned.1.call-done = bf16[512,64,128]{2,1,0:T(8,128)(2,1)} async-done(((bf16[16,64,128]{2,1,0:T(8,128)(2,1)}), bf16[512,64,128]{2,1,0:T(8,128)(2,1)}) %all-gather.9.cloned.1.call-update) | async-done | bytes 8388624 | tf_op jit(solution)/shard_map/all_gather | solution.py:47
  187.5 4.9 %gather_fusion.3 = bf16[48,64,128]{2,1,0:T(8,128)(2,1)} fusion(bf16[512,64,128]{2,1,0:T(8,128)(2,1)} %all-gather.9.cloned.1.call-done, s32[1024]{0:T(1024)S(1)} %pad_clamp_fusion), kind=kCustom, calls=%fused_computation.3 | custom fusion | bytes 1573056 | tf_op jit(solution)/shard_map/gather | solution.py:48
  192.5 3.3 %fusion.9 = f32[16,64,128]{2,1,0:T(8,128)} fusion(bf16[2,16,3,128,128]{4,3,2,1,0:T(8,128)(2,1)} %param.10, bf16[16,3,64,128]{3,2,1,0:T(8,128)(2,1)S(1)} %bitcast.65, bf16[16,3,64,128]{3,2,1,0:T(8,128)(2,1)} %bitcast.66, pred[16,3]{1,0:T(8,128)(4,1)S(1)} %bitcast.68, pred[16,3]{1,0:T(8,128)(4,1)S(1)} %copy.30), kind=kOutput, calls=%fused_computation.12 | convolution fusion | flops 101449728 | bytes 3670112 | tf_op jit(solution)/shard_map/rjcb,rjpb->rpc/dot_general | solution.py:18
  195.8 0.0 all-gather.13.cloned.1.call-update
  195.8 54.6 %all-gather.13.cloned.1.call-done = f32[128,64,128]{2,1,0:T(8,128)} async-done(((f32[16,64,128]{2,1,0:T(8,128)}), f32[128,64,128]{2,1,0:T(8,128)}) %all-gather.13.cloned.1.call-update) | async-done | bytes 4194320 | tf_op jit(solution)/shard_map/all_gather | solution.py:22
  250.5 2.6 reduce_sum.19
  253.1 3.2 %convolution_bitcast_fusion = f32[1,16,64,128]{3,2,1,0:T(8,128)S(1)} fusion(f32[2,16,128,128]{3,2,1,0:T(8,128)S(1)} %copy-done, f32[16,64,128]{2,1,0:T(8,128)S(1)} %reduce_sum.19, f32[2,16,64,128]{3,2,1,0:T(8,128)} %param.12), kind=kOutput, calls=%fused_computation.13 | convolution fusion | flops 201457664 | bytes 2621440 | tf_op jit(solution)/shard_map/rpb,rcb->rpc/dot_general | solution.py:8
  256.3 1.1 pad_maximum_fusion
  (10 shorter events, 0.1 us)
Async XLA Ops:
  6.5 57.1 %all-gather.7.cloned.1.call-start = ((), (), s32[]{:S(2)}) async-start(), calls=%async_computation | async-start | bytes 4325376 | tf_op jit(solution)/shard_map/all_gather | solution.py:32
  7.3 117.1 %all-gather.11.cloned.1.call-start = ((), (), s32[]{:S(2)}) async-start(), calls=%async_computation.2 | async-start | bytes 4718592 | tf_op jit(solution)/shard_map/all_gather | solution.py:22
  69.6 57.4 %copy-start = (f32[2,16,128,128]{3,2,1,0:T(8,128)S(1)}, f32[2,16,128,128]{3,2,1,0:T(8,128)}, u32[]{:S(2)}) copy-start(f32[2,16,128,128]{3,2,1,0:T(8,128)} %param.11) | copy-start | bytes 6291460
  69.6 117.9 %all-gather.9.cloned.1.call-start = ((), (), s32[]{:S(2)}) async-start(), calls=%async_computation.1 | async-start | bytes 8650752 | tf_op jit(solution)/shard_map/all_gather | solution.py:47
  124.4 6.9 %copy-start.2 = (s32[2,512]{1,0:T(2,128)S(1)}, s32[2,512]{1,0:T(2,128)}, u32[]{:S(2)}) copy-start(s32[2,512]{1,0:T(2,128)} %param.7) | copy-start | bytes 12292
  130.9 119.6 %all-gather.13.cloned.1.call-start = ((), (), s32[]{:S(2)}) async-start(), calls=%async_computation.3 | async-start | bytes 4718592 | tf_op jit(solution)/shard_map/all_gather | solution.py:22
  133.8 1.2 copy-start.1
Sparse Core Ops, SparseCore 0:
  9.9 53.7 all-gather.6
  69.8 54.5 all-gather.10
  131.0 56.4 all-gather.8
  196.0 54.4 all-gather.12
